TPU v7x, 256 devices: a whole 4x4x8 slice. The times are simulated.
256 devices in a mesh: gx: 32 (over y, x, core), gz: 8 (over z).
Axes of the slice: x: 4, y: 4, z: 8, core: 2. Of those that a mesh axis runs over, the one named last changes fastest.
Arguments:
- velocity: float32 [64, 3, 128, 64, 256], P(None, None, 'gx', 'gz'), may hold values from -40 to 40
- scaled_modes: float32 [64, 128, 64, 256], P(None, 'gx', 'gz'), may hold values from -70 to 70
Outputs:
- orthonormal: float32 [128, 128, 64, 256], P(None, 'gx', 'gz')
- triangle: float32 [128, 128], replicated
- lower_one: float32 [128, 128], replicated
All inputs are finite; a program needn't handle non-finite values.
Results may differ from a plain program's by a relative error of at most 0.0003.
Values sent between devices are 32-bit elements; how exact they have to be, the bound alone decides.
No kernel may reach another device: no remote copies, remote signals or barrier semaphores. Data moves between devices by JAX's collectives and lax.ppermute only.
A program may use at most 128 MiB of HBM per device.

v0:
```python
import jax
import jax.numpy as jnp
from jax import lax
from jax.sharding import PartitionSpec as P

precise = lax.Precision.HIGHEST


def with_halo(block, sides, width):
    for axis, dim in sides:
        count = lax.axis_size(axis)
        forward = [(i, i + 1) for i in range(count - 1)]
        forward.append((count - 1, 0))
        backward = [(target, source) for source, target in forward]
        low = lax.ppermute(
            lax.slice_in_dim(block, block.shape[dim] - width, None, axis=dim), axis, forward
        )
        high = lax.ppermute(lax.slice_in_dim(block, 0, width, axis=dim), axis, backward)
        block = jnp.concatenate([low, block, high], axis=dim)
    return block


def along_wall(field):
    inner = (field[..., 2:] - field[..., :-2]) * 0.5
    bottom = (-3.0 * field[..., 0:1] + 4.0 * field[..., 1:2] - field[..., 2:3]) * 0.5
    top_side = (3.0 * field[..., -1:] - 4.0 * field[..., -2:-1] + field[..., -3:-2]) * 0.5
    return jnp.concatenate([bottom, inner, top_side], -1)


def product(left, right):
    return lax.dot_general(left, right, (((1,), (1,)), ((), ())), precision=precise)


def shards(velocity, scaled_modes):
    snapshots, _, cells_x, cells_z, cells_y = velocity.shape
    columns_old = scaled_modes.shape[0]
    total_cells = cells_x * lax.axis_size("gx") * cells_z * lax.axis_size("gz") * cells_y
    mode_fields = scaled_modes.reshape(columns_old, -1)
    padded = with_halo(velocity, (("gx", 2), ("gz", 3)), 1)
    grad_x = (padded[:, :, 2:, 1:-1] - padded[:, :, :-2, 1:-1]) * 0.5
    grad_z = (padded[:, :, 1:-1, 2:] - padded[:, :, 1:-1, :-2]) * 0.5
    grad_y = along_wall(velocity)
    diagonal_part = (
        grad_x[:, 0] * grad_x[:, 0] + grad_z[:, 1] * grad_z[:, 1] + grad_y[:, 2] * grad_y[:, 2]
    )
    cross_part = (
        grad_z[:, 0] * grad_x[:, 1] + grad_y[:, 0] * grad_x[:, 2] + grad_y[:, 1] * grad_z[:, 2]
    )
    new_fields = (-0.5 * diagonal_part - cross_part).reshape(snapshots, -1)
    stacked = jnp.concatenate([mode_fields, new_fields], 0)
    gram_sum = lax.psum(product(stacked, stacked), ("gx", "gz"))
    lower_one = jnp.linalg.cholesky(gram_sum / total_cells)
    first_pass = lax.linalg.triangular_solve(lower_one, stacked, left_side=True, lower=True)
    second_sum = lax.psum(product(first_pass, first_pass), ("gx", "gz"))
    lower_two = jnp.linalg.cholesky(second_sum / total_cells)
    basis = lax.linalg.triangular_solve(lower_two, first_pass, left_side=True, lower=True)
    triangle = jnp.dot(lower_two.T, lower_one.T, precision=precise)
    return (basis.reshape(stacked.shape[0], cells_x, cells_z, cells_y), triangle, lower_one)


def solution(mesh):
    in_specs = (P(None, None, "gx", "gz", None), P(None, "gx", "gz", None))
    out_specs = (P(None, "gx", "gz", None), P(), P())
    return jax.shard_map(shards, mesh=mesh, in_specs=in_specs, out_specs=out_specs, check_vma=False)
```

profile of v0, /device:TPU:1, one launch (start us, length us, event | category | flops | bytes accessed | tf_op | source)
XLA Modules:
  0.0 683.3 jit_solution(10335882637036311948)
XLA Ops:
  7.2 6.4 copy.45
  13.7 2.7 copy-done.1
  16.3 2.0 fusion.33
  18.3 2.6 collective-permute-start.1
  21.5 7.7 %fusion.32 = (f32[64,3,4,8,1]{4,3,2,1,0:T(8,128)}, f32[64,3,4,8,1]{4,3,2,1,0:T(8,128)}, f32[64,3,4,8,1]{4,3,2,1,0:T(8,128)}, f32[64,3,4,8,1]{4,3,2,1,0:T(8,128)}...) fusion(f32[64,3,4,8,256]{4,3,2,1,0:T(8,128)S(1)} %copy-done), kind=kLoop, calls=%fused_computation.59 | loop fusion | bytes 294912 | tf_op jit(solution)/shard_map/slice | solution.py:25
  29.2 2.7 copy.66
  31.9 2.7 copy.67
  34.6 2.7 copy.68
  37.2 2.7 copy.69
  39.9 2.7 copy.70
  42.6 1.4 copy.71
  44.0 2.3 copy.57
  46.3 2.5 copy.58
  48.8 2.5 copy.72
  51.3 9.2 %fusion = f32[64,3,4,8,254]{4,0,3,2,1:T(8,128)} fusion(f32[64,3,4,8,256]{4,0,3,2,1:T(8,128)} %copy-done.1), kind=kLoop, calls=%fused_computation.1 | loop fusion | flops 3121152 | bytes 18726912 | tf_op jit(solution)/shard_map/mul | solution.py:24
  60.5 7.3 %pad_maximum_fusion.4 = f32[64,3,4,8,256]{4,0,3,2,1:T(8,128)S(1)} fusion(f32[64,3,4,8,1]{4,0,3,2,1:T(8,128)} %copy.58, f32[64,3,4,8,254]{4,0,3,2,1:T(8,128)} %fusion, f32[64,3,4,8,1]{4,0,3,2,1:T(8,128)} %copy.57), kind=kLoop, calls=%fused_computation.10 | loop fusion | flops 3145728 | bytes 12582912 | tf_op jit(solution)/shard_map/concatenate | solution.py:27
  67.8 1.5 constant_dynamic-update-slice_fusion.2
  69.3 4.1 constant_dynamic-update-slice_fusion.1
  73.4 1.7 constant_dynamic-update-slice_fusion
  75.3 5.2 collective-permute-start.2
  80.5 1.5 constant_dynamic-update-slice_fusion.4
  82.0 12.6 %fusion.4 = f32[64,3,4,8,256]{4,0,3,2,1:T(8,128)S(1)} fusion(f32[64,3,4,8,256]{4,0,3,2,1:T(8,128)S(1)} %bitcast.38, f32[64,3,1,8,256]{4,0,3,2,1:T(8,128)} %collective-permute-done.1, f32[64,3,1,8,256]{4,0,3,2,1:T(8,128)} %collective-permute-done), kind=kLoop, calls=%fused_computation.8 | loop fusion | flops 6291456 | bytes 15728640 | tf_op jit(solution)/shard_map/mul | solution.py:40
  94.5 7.4 %collective-permute-done.2 = f32[64,3,6,1,256]{4,0,3,2,1:T(8,128)S(1)} collective-permute-done((f32[64,3,6,1,256]{4,0,3,2,1:T(8,128)S(1)}, f32[64,3,6,1,256]{4,0,3,2,1:T(8,128)S(1)}, u32[]{:S(2)}, u32[]{:S(2)}) %collective-permute-start.2) | collective-permute-done | bytes 1179680 | tf_op jit(solution)/shard_map/ppermute | solution.py:18
  102.0 3.1 collective-permute-done.3
  105.1 2.1 fusion.2
  107.2 2.0 fusion.6
  109.3 2.6 copy.59
  111.8 1.7 reshape.49
  113.6 1.5 constant_dynamic-update-slice_fusion.3
  115.0 7.6 %fusion.34 = f32[128,128]{0,1:T(8,128)} fusion(f32[128,8192]{1,0:T(8,128)} %constant_dynamic-update-slice_fusion.3), kind=kOutput, calls=%fused_computation.61 | convolution fusion | flops 1610612736 | bytes 4259840 | tf_op jit(solution)/shard_map/dot_general | solution.py:31
  122.7 243.7 %all-reduce.3.cloned.1.call-done = f32[128,128]{0,1:T(8,128)} async-done(((f32[128,128]{0,1:T(8,128)}), f32[128,128]{0,1:T(8,128)}) %all-reduce.3.cloned.1.call-update) | async-done | bytes 65552 | tf_op jit(solution)/shard_map/psum | solution.py:51
  366.4 0.8 broadcast_multiply_fusion.1
  367.3 0.9 fusion.16
  368.2 11.7 %cholesky.44 = f32[128,128]{1,0:T(8,128)S(1)} custom-call(f32[128,128]{1,0:T(8,128)S(1)} %fusion.16), custom_call_target="Cholesky" | custom-call | tf_op jit(solution)/shard_map/jit(cholesky)/cholesky | solution.py:52
  380.6 0.7 fusion.20
  381.3 9.8 %custom-call.6 = f32[1,128,128]{1,2,0:T(8,128)S(1)} custom-call(f32[1,128,128]{2,1,0:T(8,128)S(1)} %get-tuple-element.5), custom_call_target="InvertDiagBlocksLowerTriangular" | custom-call | tf_op jit(solution)/shard_map/triangular_solve/custom-call.0 | solution.py:53
  391.1 5.7 fusion.14
  396.8 2.0 copy-done.2
  398.8 4.0 fusion.35
  402.8 237.9 %all-reduce.5.cloned.1.call-done = f32[128,128]{0,1:T(8,128)} async-done(((f32[128,128]{0,1:T(8,128)}), f32[128,128]{0,1:T(8,128)}) %all-reduce.5.cloned.1.call-update) | async-done | bytes 65552 | tf_op jit(solution)/shard_map/psum | solution.py:54
  640.7 0.8 broadcast_multiply_fusion
  641.6 0.9 fusion.13
  642.5 11.7 %cholesky.55 = f32[128,128]{1,0:T(8,128)S(1)} custom-call(f32[128,128]{1,0:T(8,128)S(1)} %fusion.13), custom_call_target="Cholesky" | custom-call | tf_op jit(solution)/shard_map/jit(cholesky)/cholesky | solution.py:55
  654.3 0.7 compare_reduce_fusion
  655.6 1.6 fusion.23
  657.1 9.8 %custom-call.7 = f32[1,128,128]{1,2,0:T(8,128)S(1)} custom-call(f32[1,128,128]{2,1,0:T(8,128)S(1)} %select_bitcast_fusion), custom_call_target="InvertDiagBlocksLowerTriangular" | custom-call | tf_op jit(solution)/shard_map/triangular_solve/custom-call.0 | solution.py:56
  667.0 5.7 fusion.11
  672.7 3.3 copy.73
  (37 shorter events, 2.6 us)
Async XLA Ops:
  7.2 359.2 %all-reduce.3.cloned.1.call-start = ((), (), s32[]{:S(2)}) async-start(), calls=%async_computation | async-start | bytes 131072 | tf_op jit(solution)/shard_map/psum | solution.py:51
  13.6 2.7 copy-start.1
  16.3 5.2 copy-start
  18.3 49.5 %collective-permute-start.1 = (f32[64,3,1,8,256]{4,0,3,2,1:T(8,128)}, f32[64,3,1,8,256]{4,0,3,2,1:T(8,128)}, u32[]{:S(2)}, u32[]{:S(2)}) collective-permute-start(f32[64,3,1,8,256]{4,0,3,2,1:T(8,128)} %get-tuple-element.16), channel_id=1, source_target_pairs={{0,8},{8,16},{16,24},{24,32},{32,40},{40,48},{48,56},{56,64},{64,7... | collective-permute-start | bytes 4718600 | tf_op jit(solution)/shard_map/ppermute | solution.py:15
  20.9 52.5 %collective-permute-start = (f32[64,3,1,8,256]{4,0,3,2,1:T(8,128)}, f32[64,3,1,8,256]{4,0,3,2,1:T(8,128)}, u32[]{:S(2)}, u32[]{:S(2)}) collective-permute-start(f32[64,3,1,8,256]{4,0,3,2,1:T(8,128)} %get-tuple-element.15), channel_id=1, source_target_pairs={{8,0},{16,8},{24,16},{32,24},{40,32},{48,40},{56,48},{64,56},{72,6... | collective-permute-start | bytes 4718600 | tf_op jit(solution)/shard_map/ppermute | solution.py:18
  44.0 4.8 copy-start.4
  51.3 18.0 %slice-start = ((s8[6291456]{0:T(1024)(128)(4,1)}), s8[4194304]{0:T(1024)(128)(4,1)S(1)}, s32[]{:S(2)}) async-start(s8[6291456]{0:T(1024)(128)(4,1)} %bitcast.35), calls=%async_computation.2 | async-start | bytes 8388608
  60.5 8.8 %slice-start.1 = ((s8[6291456]{0:T(1024)(128)(4,1)}), s8[2097152]{0:T(1024)(128)(4,1)S(1)}, s32[]{:S(2)}) async-start(s8[6291456]{0:T(1024)(128)(4,1)} %bitcast.35), calls=%async_computation.3 | async-start | bytes 4194304
  73.4 7.1 %copy-start.3 = (f32[8,8,32,256]{3,1,2,0:T(8,128)S(1)}, f32[8,8,32,256]{3,1,2,0:T(8,128)}, u32[]{:S(2)}) copy-start(f32[8,8,32,256]{3,1,2,0:T(8,128)} %copy.72) | copy-start | bytes 6291460
  73.4 8.6 %slice-start.2 = ((s8[6291456]{0:T(1024)(128)(4,1)}), s8[4194304]{0:T(1024)(128)(4,1)S(1)}, s32[]{:S(2)}) async-start(s8[6291456]{0:T(1024)(128)(4,1)} %bitcast.37), calls=%async_computation.4 | async-start | bytes 8388608
  75.1 6.9 %slice-start.3 = ((s8[6291456]{0:T(1024)(128)(4,1)}), s8[2097152]{0:T(1024)(128)(4,1)S(1)}, s32[]{:S(2)}) async-start(s8[6291456]{0:T(1024)(128)(4,1)} %bitcast.37), calls=%async_computation.5 | async-start | bytes 4194304
  75.3 26.6 %collective-permute-start.2 = (f32[64,3,6,1,256]{4,0,3,2,1:T(8,128)S(1)}, f32[64,3,6,1,256]{4,0,3,2,1:T(8,128)S(1)}, u32[]{:S(2)}, u32[]{:S(2)}) collective-permute-start(f32[64,3,6,1,256]{4,0,3,2,1:T(8,128)S(1)} %get-tuple-element.7), channel_id=1, source_target_pairs={{1,0},{2,1},{3,2},{4,3},{5,4},{6,5},{7,6},{0,7},{9,8},{10,9},{11,1... | collective-permute-start | bytes 3538952 | tf_op jit(solution)/shard_map/ppermute | solution.py:18
  80.5 24.6 %collective-permute-start.3 = (f32[64,3,6,1,256]{4,0,3,2,1:T(8,128)S(1)}, f32[64,3,6,1,256]{4,0,3,2,1:T(8,128)S(1)}, u32[]{:S(2)}, u32[]{:S(2)}) collective-permute-start(f32[64,3,6,1,256]{4,0,3,2,1:T(8,128)S(1)} %get-tuple-element.8), channel_id=1, source_target_pairs={{0,1},{1,2},{2,3},{3,4},{4,5},{5,6},{6,7},{7,0},{8,9},{9,10},{10,1... | collective-permute-start | bytes 3538952 | tf_op jit(solution)/shard_map/ppermute | solution.py:15
  122.7 518.0 %all-reduce.5.cloned.1.call-start = ((), (), s32[]{:S(2)}) async-start(), calls=%async_computation.1 | async-start | bytes 131072 | tf_op jit(solution)/shard_map/psum | solution.py:54
  381.3 274.3 %copy-start.5 = (f32[128,128]{1,0:T(8,128)}, f32[128,128]{1,0:T(8,128)S(1)}, u32[]{:S(2)}) copy-start(f32[128,128]{1,0:T(8,128)S(1)} %get-tuple-element.6) | copy-start | bytes 196612
  396.7 2.0 copy-start.2
Sparse Core Ops, SparseCore 0:
  122.8 243.5 all-reduce.2
  402.9 237.7 all-reduce.4
where the time goes:
time: 692 us; the launch traced here: 683 us
  waiting for transfers between devices  492 us (71%)
  other arithmetic  82.3 us (12%)
  local copies, waits for them, and re-layouts  61 us (9%)
  matrix products  24.5 us (4%)
  between operations  14.8 us (2%)
  starting transfers between devices  8.45 us (1%)
    psum x1, waiting for transfers between devices, shards(): gram_sum = lax.psum(product(stacked, stacked), ('gx', 'gz'))  244 us
    psum x1, waiting for transfers between devices, shards(): second_sum = lax.psum(product(first_pass, first_pass), ('gx', 'gz'))  238 us
    unnamed x32, local copies, waits for them, and re-layouts  38.8 us
  transfers between devices with their start and end apart: 6, of which 4 were waited for; matrix products, arithmetic and copies ran while one was open for 10% of the time, Pallas kernels for 0%

commit v1 on v0

--- a/solution.py
+++ b/solution.py
@@ -51,7 +51,9 @@
     gram_sum = lax.psum(product(stacked, stacked), ("gx", "gz"))
     lower_one = jnp.linalg.cholesky(gram_sum / total_cells)
     first_pass = lax.linalg.triangular_solve(lower_one, stacked, left_side=True, lower=True)
-    second_sum = lax.psum(product(first_pass, first_pass), ("gx", "gz"))
+    second_sum = product(first_pass, first_pass)
+    for over in ("gz", "gx"):
+        second_sum = lax.psum(second_sum, over)
     lower_two = jnp.linalg.cholesky(second_sum / total_cells)
     basis = lax.linalg.triangular_solve(lower_two, first_pass, left_side=True, lower=True)
     triangle = jnp.dot(lower_two.T, lower_one.T, precision=precise)

time: 692 us -> 631 us (0.912)
  waiting for transfers between devices: 492 us -> 441 us
  other arithmetic: 82.3 us -> 72.6 us
    psum x1 -> x2, waiting for transfers between devices: 238 us -> 178 us  [shards(): second_sum = lax.psum(second_sum, over)]
    mul x1, other arithmetic: 12.6 us -> 2.81 us  [shards(): grad_x = (padded[:, :, 2:, 1:-1] - padded[:, :, :-2, 1:-1]) * 0.5]
    ppermute x2, waiting for transfers between devices: 7.44 us -> 17.2 us  [with_halo(): lax.ppermute(lax.slice_in_dim(block, 0, width, axis=dim), axis, backward)]
  transfers between devices with their start and end apart: 6 -> 7, of which waited for: 4 -> 5; matrix products, arithmetic and copies ran while one was open for 10% -> 9% of each run, Pallas kernels for 0% -> 0%
where the time goes in v1:
time: 631 us; the launch traced here: 622 us
  waiting for transfers between devices  441 us (70%)
  other arithmetic  72.6 us (12%)
  local copies, waits for them, and re-layouts  61 us (10%)
  matrix products  24.1 us (4%)
  between operations  14.2 us (2%)
  starting transfers between devices  9.07 us (1%)
    psum x1, waiting for transfers between devices, shards(): gram_sum = lax.psum(product(stacked, stacked), ('gx', 'gz'))  243 us
    psum x2, waiting for transfers between devices, shards(): second_sum = lax.psum(second_sum, over)  178 us
    unnamed x32, local copies, waits for them, and re-layouts  38.8 us
    ppermute x2, waiting for transfers between devices, with_halo(): lax.ppermute(lax.slice_in_dim(block, 0, width, axis=dim), axis, backward)  17.2 us
  transfers between devices with their start and end apart: 7, of which 5 were waited for; matrix products, arithmetic and copies ran while one was open for 9% of the time, Pallas kernels for 0%

profile of v1, /device:TPU:1, one launch (start us, length us, event | category | flops | bytes accessed | tf_op | source)
XLA Modules:
  0.0 622.3 jit_solution(9522366315484075417)
XLA Ops:
  7.2 6.4 %copy.45 = f32[64,3,4,8,256]{4,0,3,2,1:T(8,128)S(1)} copy(f32[64,3,4,8,256]{4,3,2,1,0:T(8,128)} %param.5) | data formatting | bytes 12582912 | tf_op args[0]
  13.7 2.7 copy-done.1
  16.3 2.0 fusion.33
  18.3 2.6 collective-permute-start.1
  21.5 7.7 %fusion.32 = (f32[64,3,4,8,1]{4,3,2,1,0:T(8,128)}, f32[64,3,4,8,1]{4,3,2,1,0:T(8,128)}, f32[64,3,4,8,1]{4,3,2,1,0:T(8,128)}, f32[64,3,4,8,1]{4,3,2,1,0:T(8,128)}...) fusion(f32[64,3,4,8,256]{4,3,2,1,0:T(8,128)S(1)} %copy-done), kind=kLoop, calls=%fused_computation.59 | loop fusion | bytes 294912 | tf_op jit(solution)/shard_map/slice | solution.py:25
  29.2 2.7 copy.66
  31.9 2.7 copy.67
  34.6 2.7 copy.68
  37.2 2.7 copy.69
  39.9 2.7 copy.70
  42.6 1.4 copy.71
  44.0 2.3 copy.57
  46.3 2.4 copy.58
  48.7 2.5 copy.72
  51.2 9.2 %fusion = f32[64,3,4,8,254]{4,0,3,2,1:T(8,128)} fusion(f32[64,3,4,8,256]{4,0,3,2,1:T(8,128)} %copy-done.1), kind=kLoop, calls=%fused_computation.1 | loop fusion | flops 3121152 | bytes 18726912 | tf_op jit(solution)/shard_map/mul | solution.py:24
  60.4 7.3 %pad_maximum_fusion.4 = f32[64,3,4,8,256]{4,0,3,2,1:T(8,128)S(1)} fusion(f32[64,3,4,8,1]{4,0,3,2,1:T(8,128)} %copy.58, f32[64,3,4,8,254]{4,0,3,2,1:T(8,128)} %fusion, f32[64,3,4,8,1]{4,0,3,2,1:T(8,128)} %copy.57), kind=kLoop, calls=%fused_computation.10 | loop fusion | flops 3145728 | bytes 12582912 | tf_op jit(solution)/shard_map/concatenate | solution.py:27
  67.7 1.5 constant_dynamic-update-slice_fusion.2
  69.2 4.1 constant_dynamic-update-slice_fusion.1
  73.3 1.7 constant_dynamic-update-slice_fusion
  75.2 5.2 collective-permute-start.2
  80.4 1.5 constant_dynamic-update-slice_fusion.4
  81.9 2.8 fusion.4
  84.7 17.2 %collective-permute-done.2 = f32[64,3,6,1,256]{4,0,3,2,1:T(8,128)S(1)} collective-permute-done((f32[64,3,6,1,256]{4,0,3,2,1:T(8,128)S(1)}, f32[64,3,6,1,256]{4,0,3,2,1:T(8,128)S(1)}, u32[]{:S(2)}, u32[]{:S(2)}) %collective-permute-start.2) | collective-permute-done | bytes 1179680 | tf_op jit(solution)/shard_map/ppermute | solution.py:18
  101.9 3.1 collective-permute-done.3
  105.0 2.1 fusion.2
  107.1 2.0 fusion.6
  109.2 2.6 copy.59
  111.7 1.7 reshape.49
  113.5 1.5 constant_dynamic-update-slice_fusion.3
  115.0 7.6 %fusion.34 = f32[128,128]{0,1:T(8,128)} fusion(f32[128,8192]{1,0:T(8,128)} %constant_dynamic-update-slice_fusion.3), kind=kOutput, calls=%fused_computation.61 | convolution fusion | flops 1610612736 | bytes 4259840 | tf_op jit(solution)/shard_map/dot_general | solution.py:31
  123.0 243.2 %all-reduce.4.cloned.1.call-done = f32[128,128]{0,1:T(8,128)} async-done(((f32[128,128]{0,1:T(8,128)}), f32[128,128]{0,1:T(8,128)}) %all-reduce.4.cloned.1.call-update) | async-done | bytes 65552 | tf_op jit(solution)/shard_map/psum | solution.py:51
  366.3 0.8 broadcast_multiply_fusion.1
  367.2 0.9 fusion.16
  368.1 11.7 %cholesky.44 = f32[128,128]{1,0:T(8,128)S(1)} custom-call(f32[128,128]{1,0:T(8,128)S(1)} %fusion.16), custom_call_target="Cholesky" | custom-call | tf_op jit(solution)/shard_map/jit(cholesky)/cholesky | solution.py:52
  381.1 9.8 %custom-call.6 = f32[1,128,128]{1,2,0:T(8,128)S(1)} custom-call(f32[1,128,128]{2,1,0:T(8,128)S(1)} %get-tuple-element.5), custom_call_target="InvertDiagBlocksLowerTriangular" | custom-call | tf_op jit(solution)/shard_map/triangular_solve/custom-call.0 | solution.py:53
  391.0 5.4 fusion.14
  396.4 2.0 copy-done.2
  398.4 4.0 fusion.35
  402.7 63.5 %all-reduce.6.cloned.1.call-done = f32[128,128]{0,1:T(8,128)} async-done(((f32[128,128]{0,1:T(8,128)}), f32[128,128]{0,1:T(8,128)}) %all-reduce.6.cloned.1.call-update) | async-done | bytes 65552 | tf_op jit(solution)/shard_map/psum | solution.py:56
  466.2 114.3 %all-reduce.8.cloned.1.call-done = f32[128,128]{0,1:T(8,128)} async-done(((f32[128,128]{0,1:T(8,128)}), f32[128,128]{0,1:T(8,128)}) %all-reduce.8.cloned.1.call-update) | async-done | bytes 65552 | tf_op jit(solution)/shard_map/psum | solution.py:56
  580.6 0.8 broadcast_multiply_fusion
  581.5 0.9 fusion.13
  582.4 11.7 %cholesky.55 = f32[128,128]{1,0:T(8,128)S(1)} custom-call(f32[128,128]{1,0:T(8,128)S(1)} %fusion.13), custom_call_target="Cholesky" | custom-call | tf_op jit(solution)/shard_map/jit(cholesky)/cholesky | solution.py:57
  594.1 0.7 compare_reduce_fusion
  595.4 1.6 fusion.23
  597.0 9.8 %custom-call.7 = f32[1,128,128]{1,2,0:T(8,128)S(1)} custom-call(f32[1,128,128]{2,1,0:T(8,128)S(1)} %select_bitcast_fusion), custom_call_target="InvertDiagBlocksLowerTriangular" | custom-call | tf_op jit(solution)/shard_map/triangular_solve/custom-call.0 | solution.py:58
  606.8 5.4 fusion.11
  612.2 3.3 copy.73
  (40 shorter events, 3.8 us)
Async XLA Ops:
  7.2 359.1 %all-reduce.4.cloned.1.call-start = ((), (), s32[]{:S(2)}) async-start(), calls=%async_computation | async-start | bytes 131072 | tf_op jit(solution)/shard_map/psum | solution.py:51
  13.6 2.7 copy-start.1
  16.3 5.2 copy-start
  18.3 49.4 %collective-permute-start.1 = (f32[64,3,1,8,256]{4,0,3,2,1:T(8,128)}, f32[64,3,1,8,256]{4,0,3,2,1:T(8,128)}, u32[]{:S(2)}, u32[]{:S(2)}) collective-permute-start(f32[64,3,1,8,256]{4,0,3,2,1:T(8,128)} %get-tuple-element.16), channel_id=1, source_target_pairs={{0,8},{8,16},{16,24},{24,32},{32,40},{40,48},{48,56},{56,64},{64,7... | collective-permute-start | bytes 4718600 | tf_op jit(solution)/shard_map/ppermute | solution.py:15
  20.9 52.4 %collective-permute-start = (f32[64,3,1,8,256]{4,0,3,2,1:T(8,128)}, f32[64,3,1,8,256]{4,0,3,2,1:T(8,128)}, u32[]{:S(2)}, u32[]{:S(2)}) collective-permute-start(f32[64,3,1,8,256]{4,0,3,2,1:T(8,128)} %get-tuple-element.15), channel_id=1, source_target_pairs={{8,0},{16,8},{24,16},{32,24},{40,32},{48,40},{56,48},{64,56},{72,6... | collective-permute-start | bytes 4718600 | tf_op jit(solution)/shard_map/ppermute | solution.py:18
  44.0 4.7 copy-start.4
  51.2 18.0 %slice-start = ((s8[6291456]{0:T(1024)(128)(4,1)}), s8[4194304]{0:T(1024)(128)(4,1)S(1)}, s32[]{:S(2)}) async-start(s8[6291456]{0:T(1024)(128)(4,1)} %bitcast.35), calls=%async_computation.3 | async-start | bytes 8388608
  60.4 8.8 %slice-start.1 = ((s8[6291456]{0:T(1024)(128)(4,1)}), s8[2097152]{0:T(1024)(128)(4,1)S(1)}, s32[]{:S(2)}) async-start(s8[6291456]{0:T(1024)(128)(4,1)} %bitcast.35), calls=%async_computation.4 | async-start | bytes 4194304
  73.3 7.1 %copy-start.3 = (f32[8,8,32,256]{3,1,2,0:T(8,128)S(1)}, f32[8,8,32,256]{3,1,2,0:T(8,128)}, u32[]{:S(2)}) copy-start(f32[8,8,32,256]{3,1,2,0:T(8,128)} %copy.72) | copy-start | bytes 6291460
  73.3 8.6 %slice-start.2 = ((s8[6291456]{0:T(1024)(128)(4,1)}), s8[4194304]{0:T(1024)(128)(4,1)S(1)}, s32[]{:S(2)}) async-start(s8[6291456]{0:T(1024)(128)(4,1)} %bitcast.37), calls=%async_computation.5 | async-start | bytes 8388608
  75.0 6.9 %slice-start.3 = ((s8[6291456]{0:T(1024)(128)(4,1)}), s8[2097152]{0:T(1024)(128)(4,1)S(1)}, s32[]{:S(2)}) async-start(s8[6291456]{0:T(1024)(128)(4,1)} %bitcast.37), calls=%async_computation.6 | async-start | bytes 4194304
  75.2 26.6 %collective-permute-start.2 = (f32[64,3,6,1,256]{4,0,3,2,1:T(8,128)S(1)}, f32[64,3,6,1,256]{4,0,3,2,1:T(8,128)S(1)}, u32[]{:S(2)}, u32[]{:S(2)}) collective-permute-start(f32[64,3,6,1,256]{4,0,3,2,1:T(8,128)S(1)} %get-tuple-element.7), channel_id=1, source_target_pairs={{1,0},{2,1},{3,2},{4,3},{5,4},{6,5},{7,6},{0,7},{9,8},{10,9},{11,1... | collective-permute-start | bytes 3538952 | tf_op jit(solution)/shard_map/ppermute | solution.py:18
  80.4 24.6 %collective-permute-start.3 = (f32[64,3,6,1,256]{4,0,3,2,1:T(8,128)S(1)}, f32[64,3,6,1,256]{4,0,3,2,1:T(8,128)S(1)}, u32[]{:S(2)}, u32[]{:S(2)}) collective-permute-start(f32[64,3,6,1,256]{4,0,3,2,1:T(8,128)S(1)} %get-tuple-element.8), channel_id=1, source_target_pairs={{0,1},{1,2},{2,3},{3,4},{4,5},{5,6},{6,7},{7,0},{8,9},{9,10},{10,1... | collective-permute-start | bytes 3538952 | tf_op jit(solution)/shard_map/ppermute | solution.py:15
  122.6 343.6 %all-reduce.6.cloned.1.call-start = ((), (), s32[]{:S(2)}) async-start(), calls=%async_computation.1 | async-start | bytes 131072 | tf_op jit(solution)/shard_map/psum | solution.py:56
  381.1 214.3 %copy-start.5 = (f32[128,128]{1,0:T(8,128)}, f32[128,128]{1,0:T(8,128)S(1)}, u32[]{:S(2)}) copy-start(f32[128,128]{1,0:T(8,128)S(1)} %get-tuple-element.6) | copy-start | bytes 196612
  396.4 2.0 copy-start.2
  402.5 178.1 %all-reduce.8.cloned.1.call-start = ((), (), s32[]{:S(2)}) async-start(), calls=%async_computation.2 | async-start | bytes 131072 | tf_op jit(solution)/shard_map/psum | solution.py:56
Sparse Core Ops, SparseCore 0:
  122.7 243.5 all-reduce.3
  402.6 63.5 all-reduce.5
  469.5 111.0 all-reduce.7
